TPU v7x, 128 devices: a whole 4x4x4 slice. The times are simulated.
128 devices in a mesh: row: 16 (over z, y), col: 8 (over x, core).
Axes of the slice: x: 4, y: 4, z: 4, core: 2. Of those that a mesh axis runs over, the one named last changes fastest.
Arguments:
- amplitudes: bfloat16 [16, 4, 1024, 1024], P(None, None, 'row', 'col'), may hold values from -6 to 6
- cycle_integrals: bfloat16 [4, 8, 1024, 1024], P(None, None, 'row', 'col'), may hold values from -0.375 to 0.375
- mask_amp: int32 [16, 16], replicated, may hold values 0 or 1
- mask_int: int32 [16, 16], replicated, may hold values 0 or 1
- occupied_i: float32 [16], P('row'), may hold values from -1 to -0.3
- occupied_j: float32 [8], P('col'), may hold values from -1 to -0.3
- virtual_energy: float32 [1024], replicated, may hold values from 0.2 to 1.5
Outputs:
- update: bfloat16 [16, 8, 1024, 1024], P('row', 'col')
Inputs may be any that keep to these rules, and one draw needn't show every extreme that they name: mask_amp holds 0 or 1: 1 where the amplitude tile survives screening. mask_int holds 0 or 1: 1 where the intermediate tile survives screening.
All inputs are finite; a program needn't handle non-finite values.
Results may differ from a plain program's by a relative error of at most 0.0049.
Values may be sent and summed in bfloat16 or wider, within the bound.
A program may use at most 192 MiB of HBM per device.

v0:
```python
import jax
import jax.numpy as jnp
from jax import lax
from jax.sharding import PartitionSpec as P

TILE = 64


def local_mask(mask, row_first, row_tiles, col_first, col_tiles):
    window = lax.dynamic_slice(mask, (row_first, col_first), (row_tiles, col_tiles))
    return jnp.repeat(jnp.repeat(window, TILE, axis=0), TILE, axis=1).astype(jnp.bfloat16)


def per_device(
    amplitudes, cycle_integrals, mask_amp, mask_int, occupied_i, occupied_j, virtual_energy
):
    row_index = lax.axis_index("row")
    col_index = lax.axis_index("col")
    row_tiles = amplitudes.shape[2] // TILE
    col_tiles = amplitudes.shape[3] // TILE
    amp_masked = (
        amplitudes
        * local_mask(mask_amp, row_index * row_tiles, row_tiles, col_index * col_tiles, col_tiles)[
            None, None
        ]
    )
    int_masked = (
        cycle_integrals
        * local_mask(mask_int, row_index * row_tiles, row_tiles, col_index * col_tiles, col_tiles)[
            None, None
        ]
    )
    whole = virtual_energy.shape[0]
    partial_value = jnp.einsum(
        "ikac,kjbc->ijab",
        amp_masked,
        lax.all_gather(int_masked, "row", axis=2, tiled=True),
        preferred_element_type=jnp.float32,
    )
    exchanged = lax.all_to_all(
        lax.all_to_all(partial_value[None], "row", split_axis=1, concat_axis=3, tiled=True),
        "col",
        split_axis=2,
        concat_axis=0,
        tiled=True,
    )
    cycle = jnp.sum(exchanged, axis=0).astype(jnp.bfloat16)
    denominator = virtual_energy[:, None] + virtual_energy[None, :] - occupied_i[0] - occupied_j[0]
    result = cycle.reshape(whole, whole).astype(jnp.float32) / denominator
    return result.astype(jnp.bfloat16)[None, None]


def solution(mesh):
    in_specs = (
        P(None, None, "row", "col"),
        P(None, None, "row", "col"),
        P(),
        P(),
        P("row"),
        P("col"),
        P(),
    )
    out_specs = P("row", "col", None, None)
    return jax.shard_map(
        per_device, mesh=mesh, in_specs=in_specs, out_specs=out_specs, check_vma=False
    )
```

profile of v0, /device:TPU:1, one launch (start us, length us, event | category | flops | bytes accessed | tf_op | source)
XLA Modules:
  0.0 901.8 jit_solution(1429564766172475192)
XLA Ops:
  6.5 0.0 all-gather.2.cloned.1.call-start
  6.5 0.8 convert_bitcast_fusion
  7.3 0.1 broadcast_in_dim.6
  7.4 0.1 convert_element_type.63
  7.5 1.9 copy_multiply_fusion
  9.4 0.0 all-gather.2.cloned.1.call-update
  9.4 0.1 broadcast_in_dim.7
  9.4 0.1 convert_element_type.66
  9.5 74.1 %all-gather.2.cloned.1.call-done = bf16[4,8,1024,128]{3,2,0,1:T(8,128)(2,1)} async-done(((bf16[4,8,64,128]{3,2,0,1:T(8,128)(2,1)}), bf16[4,8,1024,128]{3,2,0,1:T(8,128)(2,1)}) %all-gather.2.cloned.1.call-update) | async-done | bytes 8388624 | tf_op jit(solution)/shard_map/all_gather | solution.py:37
  83.6 18.9 %convolution_bitcast_fusion = f32[1,16,8,64,1024]{4,3,1,2,0:T(8,128)} fusion(bf16[4,8,1024,128]{3,2,0,1:T(8,128)(2,1)} %all-gather.2.cloned.1.call-done, bf16[16,4,64,128]{3,2,1,0:T(8,128)(2,1)} %param.7, bf16[128]{0:T(256)(128)(2,1)S(1)} %convert_element_type.66), kind=kOutput, calls=%fused_computation | convolution fusion | flops 8592031744 | bytes 42991872 | tf_op jit(solution)/shard_map/ikac,kjbc->ijab/dot_general | solution.py:34
  102.5 12.1 %copy.12 = f32[1,16,8,64,1024]{4,3,2,0,1:T(8,128)S(1)} copy(f32[1,16,8,64,1024]{4,3,1,2,0:T(8,128)} %convolution_bitcast_fusion) | data formatting | bytes 67108864 | tf_op jit(solution)/shard_map/broadcast_in_dim | solution.py:41
  114.6 369.3 %all_to_all.27 = f32[1,16,8,64,1024]{4,3,2,0,1:T(8,128)} all-to-all(f32[1,16,8,64,1024]{4,3,2,0,1:T(8,128)S(1)} %copy.12), channel_id=1, replica_groups=mesh['row'=16,'col'=8] {'row'}, dimensions={1} | all-to-all | bytes 67108864 | tf_op jit(solution)/shard_map/all_to_all | solution.py:41
  483.9 23.3 %copy.13 = f32[1,16,8,64,1024]{4,3,1,2,0:T(8,128)} copy(f32[1,16,8,64,1024]{4,3,2,0,1:T(8,128)} %all_to_all.27) | data formatting | bytes 67108864 | tf_op jit(solution)/shard_map/all_to_all | solution.py:41
  507.3 9.0 %all-to-all-start.1 = ((f32[1,1,8,1024,1024]{4,3,1,0,2:T(8,128)}), f32[1,1,8,1024,1024]{4,3,1,0,2:T(8,128)}, u32[]{:S(2)}, u32[]{:S(2)}) async-start(f32[1,1,8,1024,1024]{4,3,1,0,2:T(8,128)} %bitcast.33), calls=%async_computation.1 | async-start | bytes 67108864 | tf_op jit(solution)/shard_map/all_to_all | solution.py:40
  517.6 0.0 copy-start
  517.6 362.2 %all-to-all-done.1 = f32[1,1,8,1024,1024]{4,3,1,0,2:T(8,128)} async-done(((f32[1,1,8,1024,1024]{4,3,1,0,2:T(8,128)}), f32[1,1,8,1024,1024]{4,3,1,0,2:T(8,128)}, u32[]{:S(2)}, u32[]{:S(2)}) %all-to-all-start.1) | async-done | bytes 33554464 | tf_op jit(solution)/shard_map/all_to_all | solution.py:40
  879.8 12.9 %reduce_sum.9 = bf16[1024,1024]{1,0:T(8,128)(2,1)S(1)} reduce(f32[1,1,8,1024,1024]{4,3,1,0,2:T(8,128)} %all-to-all-done.1, f32[]{:T(128)} %constant.16.clone.1), dimensions={0,1,2}, to_apply=%region_0.0 | reduce | flops 7340032 | bytes 35651588 | tf_op jit(solution)/shard_map/reduce_sum | solution.py:47
  892.7 0.0 copy-done
  892.7 2.3 fusion.1
Async XLA Ops:
  6.5 77.1 %all-gather.2.cloned.1.call-start = ((), (), s32[]{:S(2)}) async-start(), calls=%async_computation.2 | async-start | bytes 8912896 | tf_op jit(solution)/shard_map/all_gather | solution.py:37
  507.3 372.6 %all-to-all-start.1 = ((f32[1,1,8,1024,1024]{4,3,1,0,2:T(8,128)}), f32[1,1,8,1024,1024]{4,3,1,0,2:T(8,128)}, u32[]{:S(2)}, u32[]{:S(2)}) async-start(f32[1,1,8,1024,1024]{4,3,1,0,2:T(8,128)} %bitcast.33), calls=%async_computation.1 | async-start | bytes 67108864 | tf_op jit(solution)/shard_map/all_to_all | solution.py:40
  517.6 375.1 %copy-start = (f32[1024]{0:T(1024)S(1)}, f32[1024]{0:T(1024)}, u32[]{:S(2)}) copy-start(f32[1024]{0:T(1024)} %param.13) | copy-start | bytes 12292
Sparse Core Ops, SparseCore 0:
  9.5 74.0 all-gather.1
where the time goes:
time: 902 us
  waiting for transfers between devices  436 us (48%)
  blocking collectives  369 us (41%)
  local copies, waits for them, and re-layouts  35.8 us (4%)
  matrix products  18.9 us (2%)
  other arithmetic  17.8 us (2%)
  between operations  14.7 us (2%)
  starting transfers between devices  9.05 us (1%)
    all_to_all x1, blocking collectives, per_device(): lax.all_to_all(partial_value[None], 'row', split_axis=1, concat_axis=3, t...  369 us
    all_to_all x1, waiting for transfers between devices, per_device(): lax.all_to_all(lax.all_to_all(partial_value[None], 'row', split_axis=1, c...  362 us
    all_gather x1, waiting for transfers between devices, per_device(): lax.all_gather(int_masked, 'row', axis=2, tiled=True)  74.1 us
    all_to_all x1, local copies, waits for them, and re-layouts, per_device(): lax.all_to_all(partial_value[None], 'row', split_axis=1, concat_axis=3, t...  23.3 us
    dot_general x1, matrix products, per_device(): jnp.einsum('ikac,kjbc->ijab', amp_masked, lax.all_gather(int_masked, 'row...  18.9 us
  transfers between devices with their start and end apart: 2, of which 2 were waited for; matrix products, arithmetic and copies ran while one was open for 0% of the time, Pallas kernels for 0%

commit v1 on v0

--- a/solution.py
+++ b/solution.py
@@ -1,9 +1,22 @@
+import functools
 import jax
 import jax.numpy as jnp
 from jax import lax
 from jax.sharding import PartitionSpec as P
 
 TILE = 64
+
+
+def _build_sums_all(raw, group_axis):
+    inbox = []
+    for _ in range(lax.axis_size(group_axis)):
+        inbox.append(raw)
+    return jnp.concatenate(
+        lax.all_to_all(jnp.stack(inbox), group_axis, split_axis=0, concat_axis=0), axis=2
+    )
+
+
+deliver_core = functools.partial(_build_sums_all, group_axis="row")
 
 
 def local_mask(mask, row_first, row_tiles, col_first, col_tiles):
@@ -32,10 +45,7 @@
     )
     whole = virtual_energy.shape[0]
     partial_value = jnp.einsum(
-        "ikac,kjbc->ijab",
-        amp_masked,
-        lax.all_gather(int_masked, "row", axis=2, tiled=True),
-        preferred_element_type=jnp.float32,
+        "ikac,kjbc->ijab", amp_masked, deliver_core(int_masked), preferred_element_type=jnp.float32
     )
     exchanged = lax.all_to_all(
         lax.all_to_all(partial_value[None], "row", split_axis=1, concat_axis=3, tiled=True),

time: 902 us -> 966 us (1.071)
  waiting for transfers between devices: 436 us -> 485 us
  local copies, waits for them, and re-layouts: 35.8 us -> 50.8 us
  between operations: 14.7 us -> 1.36 us
  starting transfers between devices: 9.05 us -> 18.8 us
    all_to_all x0 -> x1, waiting for transfers between devices: none -> 123 us  [_build_sums_all(): lax.all_to_all(jnp.stack(inbox), group_axis, split_axis=0, concat_axis=0)]
    all_gather x1 -> x0, waiting for transfers between devices: 74.1 us -> none  [per_device(): lax.all_gather(int_masked, 'row', axis=2, tiled=True)]
where the time goes in v1:
time: 966 us; the launch traced here: 965 us
  waiting for transfers between devices  485 us (50%)
  blocking collectives  374 us (39%)
  local copies, waits for them, and re-layouts  50.8 us (5%)
  starting transfers between devices  18.8 us (2%)
  matrix products  18.7 us (2%)
  other arithmetic  17 us (2%)
    all_to_all x1, blocking collectives, per_device(): lax.all_to_all(partial_value[None], 'row', split_axis=1, concat_axis=3, t...  374 us
    all_to_all x1, waiting for transfers between devices, per_device(): lax.all_to_all(lax.all_to_all(partial_value[None], 'row', split_axis=1, c...  362 us
    all_to_all x1, waiting for transfers between devices, _build_sums_all(): lax.all_to_all(jnp.stack(inbox), group_axis, split_axis=0, concat_axis=0)  123 us
    all_to_all x1, local copies, waits for them, and re-layouts, per_device(): lax.all_to_all(partial_value[None], 'row', split_axis=1, concat_axis=3, t...  23.3 us
  transfers between devices with their start and end apart: 2, of which 2 were waited for; matrix products, arithmetic and copies ran while one was open for 0% of the time, Pallas kernels for 0%

profile of v1, /device:TPU:1, one launch (start us, length us, event | category | flops | bytes accessed | tf_op | source)
XLA Modules:
  0.0 965.3 jit_solution(559311313463763385)
XLA Ops:
  0.0 0.8 convert_bitcast_fusion
  0.8 0.1 broadcast_in_dim.6
  0.9 0.1 convert_element_type.63
  0.9 1.1 broadcast_multiply_fusion
  2.1 5.4 stack.2
  7.4 8.6 all-to-all-start
  16.1 0.1 broadcast_in_dim.7
  16.2 0.1 convert_element_type.66
  16.2 123.0 %all-to-all-done = bf16[16,4,8,64,128]{4,3,1,2,0:T(8,128)(2,1)} async-done(((bf16[16,4,8,64,128]{4,3,1,2,0:T(8,128)(2,1)}), bf16[16,4,8,64,128]{4,3,1,2,0:T(8,128)(2,1)}, u32[]{:S(2)}, u32[]{:S(2)}) %all-to-all-start) | async-done | bytes 8388640 | tf_op jit(solution)/shard_map/all_to_all | solution.py:15
  139.2 0.0 copy-start.1
  139.2 9.7 %copy.13 = bf16[4,8,16,64,128]{4,3,2,0,1:T(8,128)(2,1)} copy(bf16[4,8,16,64,128]{4,3,0,1,2:T(8,128)(2,1)} %bitcast.1) | data formatting | bytes 16777216 | tf_op jit(solution)/shard_map/reshape | solution.py:14
  148.9 0.0 copy-done.1
  148.9 18.7 %convolution_bitcast_fusion = f32[1,16,8,64,1024]{4,3,1,2,0:T(8,128)} fusion(bf16[4,8,1024,128,1]{3,2,0,4,1:T(8,128)(2,1)} %bitcast.36, bf16[16,4,64,128]{3,2,1,0:T(8,128)(2,1)S(1)} %copy-done.1, bf16[128]{0:T(256)(128)(2,1)S(1)} %convert_element_type.66), kind=kOutput, calls=%fused_computation | convolution fusion | flops 8592031744 | bytes 42991872 | tf_op jit(solution)/shard_map/ikac,kjbc->ijab/dot_general | solution.py:47
  167.6 12.1 %copy.14 = f32[1,16,8,64,1024]{4,3,2,0,1:T(8,128)S(1)} copy(f32[1,16,8,64,1024]{4,3,1,2,0:T(8,128)} %convolution_bitcast_fusion) | data formatting | bytes 67108864 | tf_op jit(solution)/shard_map/broadcast_in_dim | solution.py:51
  179.7 373.5 %all_to_all.32 = f32[1,16,8,64,1024]{4,3,2,0,1:T(8,128)} all-to-all(f32[1,16,8,64,1024]{4,3,2,0,1:T(8,128)S(1)} %copy.14), channel_id=1, replica_groups=mesh['row'=16,'col'=8] {'row'}, dimensions={1} | all-to-all | bytes 67108864 | tf_op jit(solution)/shard_map/all_to_all | solution.py:51
  553.2 23.3 %copy.15 = f32[1,16,8,64,1024]{4,3,1,2,0:T(8,128)} copy(f32[1,16,8,64,1024]{4,3,2,0,1:T(8,128)} %all_to_all.32) | data formatting | bytes 67108864 | tf_op jit(solution)/shard_map/all_to_all | solution.py:51
  576.5 10.1 %all-to-all-start.2 = ((f32[1,1,8,1024,1024]{4,3,1,0,2:T(8,128)}), f32[1,1,8,1024,1024]{4,3,1,0,2:T(8,128)}, u32[]{:S(2)}, u32[]{:S(2)}) async-start(f32[1,1,8,1024,1024]{4,3,1,0,2:T(8,128)} %bitcast.35), calls=%async_computation.2 | async-start | bytes 67108864 | tf_op jit(solution)/shard_map/all_to_all | solution.py:50
  587.9 0.0 copy-start
  588.0 362.2 %all-to-all-done.2 = f32[1,1,8,1024,1024]{4,3,1,0,2:T(8,128)} async-done(((f32[1,1,8,1024,1024]{4,3,1,0,2:T(8,128)}), f32[1,1,8,1024,1024]{4,3,1,0,2:T(8,128)}, u32[]{:S(2)}, u32[]{:S(2)}) %all-to-all-start.2) | async-done | bytes 33554464 | tf_op jit(solution)/shard_map/all_to_all | solution.py:50
  950.2 12.9 %reduce_sum.9 = bf16[1024,1024]{1,0:T(8,128)(2,1)S(1)} reduce(f32[1,1,8,1024,1024]{4,3,1,0,2:T(8,128)} %all-to-all-done.2, f32[]{:T(128)} %constant.16.clone.1), dimensions={0,1,2}, to_apply=%region_0.0 | reduce | flops 7340032 | bytes 35651588 | tf_op jit(solution)/shard_map/reduce_sum | solution.py:57
  963.0 0.0 copy-done
  963.0 2.3 fusion
  (1 shorter events, 0.0 us)
Async XLA Ops:
  7.4 131.8 %all-to-all-start = ((bf16[16,4,8,64,128]{4,3,1,2,0:T(8,128)(2,1)}), bf16[16,4,8,64,128]{4,3,1,2,0:T(8,128)(2,1)}, u32[]{:S(2)}, u32[]{:S(2)}) async-start(bf16[16,4,8,64,128]{4,3,1,2,0:T(8,128)(2,1)} %stack.2), calls=%async_computation | async-start | bytes 16777216 | tf_op jit(solution)/shard_map/all_to_all | solution.py:15
  139.2 9.7 %copy-start.1 = (bf16[16,4,64,128]{3,2,1,0:T(8,128)(2,1)S(1)}, bf16[16,4,64,128]{3,2,1,0:T(8,128)(2,1)}, u32[]{:S(2)}) copy-start(bf16[16,4,64,128]{3,2,1,0:T(8,128)(2,1)} %param.7) | copy-start | bytes 3145732
  576.5 373.7 %all-to-all-start.2 = ((f32[1,1,8,1024,1024]{4,3,1,0,2:T(8,128)}), f32[1,1,8,1024,1024]{4,3,1,0,2:T(8,128)}, u32[]{:S(2)}, u32[]{:S(2)}) async-start(f32[1,1,8,1024,1024]{4,3,1,0,2:T(8,128)} %bitcast.35), calls=%async_computation.2 | async-start | bytes 67108864 | tf_op jit(solution)/shard_map/all_to_all | solution.py:50
  587.9 375.1 %copy-start = (f32[1024]{0:T(1024)S(1)}, f32[1024]{0:T(1024)}, u32[]{:S(2)}) copy-start(f32[1024]{0:T(1024)} %param.13) | copy-start | bytes 12292

commit v2 on v0

--- a/solution.py
+++ b/solution.py
@@ -4,6 +4,13 @@
 from jax.sharding import PartitionSpec as P
 
 TILE = 64
+
+
+def swap_blocks(x, axis, split, join):
+    size = lax.axis_size(axis)
+    parts = jnp.stack(jnp.split(x, size, axis=split), axis=0)
+    parts = lax.all_to_all(parts, axis, split_axis=0, concat_axis=0)
+    return jnp.concatenate(parts, axis=join)
 
 
 def local_mask(mask, row_first, row_tiles, col_first, col_tiles):
@@ -38,7 +45,7 @@
         preferred_element_type=jnp.float32,
     )
     exchanged = lax.all_to_all(
-        lax.all_to_all(partial_value[None], "row", split_axis=1, concat_axis=3, tiled=True),
+        swap_blocks(partial_value[None], "row", 1, 3),
         "col",
         split_axis=2,
         concat_axis=0,

time: 902 us -> 929 us (1.030)
  local copies, waits for them, and re-layouts: 35.8 us -> 62 us
    unnamed x2 -> x17, local copies, waits for them, and re-layouts: 0.01 us -> 47.5 us
    all_to_all x1 -> x0, local copies, waits for them, and re-layouts: 23.3 us -> none  [per_device(): lax.all_to_all(partial_value[None], 'row', split_axis=1, concat_axis=3, t...]
    broadcast_in_dim x1 -> x0, local copies, waits for them, and re-layouts: 12.1 us -> none  [per_device(): partial_value[None]]
    reshape x0 -> x1, local copies, waits for them, and re-layouts: none -> 11 us  [swap_blocks(): return jnp.concatenate(parts, axis=join)]
where the time goes in v2:
time: 929 us; the launch traced here: 928 us
  waiting for transfers between devices  436 us (47%)
  blocking collectives  369 us (40%)
  local copies, waits for them, and re-layouts  62 us (7%)
  matrix products  18.9 us (2%)
  other arithmetic  17.8 us (2%)
  between operations  14.7 us (2%)
    all_to_all x1, blocking collectives, swap_blocks(): parts = lax.all_to_all(parts, axis, split_axis=0, concat_axis=0)  369 us
    all_to_all x1, waiting for transfers between devices, per_device(): lax.all_to_all(swap_blocks(partial_value[None], 'row', 1, 3), 'col', spli...  362 us
    all_gather x1, waiting for transfers between devices, per_device(): lax.all_gather(int_masked, 'row', axis=2, tiled=True)  74.1 us
    unnamed x17, local copies, waits for them, and re-layouts  47.5 us
    dot_general x1, matrix products, per_device(): jnp.einsum('ikac,kjbc->ijab', amp_masked, lax.all_gather(int_masked, 'row...  18.9 us
  transfers between devices with their start and end apart: 2, of which 2 were waited for; matrix products, arithmetic and copies ran while one was open for 0% of the time, Pallas kernels for 0%

profile of v2, /device:TPU:1, one launch (start us, length us, event | category | flops | bytes accessed | tf_op | source)
XLA Modules:
  0.0 928.1 jit_solution(13373257223266775989)
XLA Ops:
  6.5 0.0 all-gather.2.cloned.1.call-start
  6.5 0.8 convert_bitcast_fusion
  7.3 0.1 broadcast_in_dim.6
  7.4 0.1 convert_element_type.63
  7.5 1.9 copy_multiply_fusion
  9.4 0.0 all-gather.2.cloned.1.call-update
  9.4 0.1 broadcast_in_dim.7
  9.4 0.1 convert_element_type.66
  9.5 74.1 %all-gather.2.cloned.1.call-done = bf16[4,8,1024,128]{3,2,0,1:T(8,128)(2,1)} async-done(((bf16[4,8,64,128]{3,2,0,1:T(8,128)(2,1)}), bf16[4,8,1024,128]{3,2,0,1:T(8,128)(2,1)}) %all-gather.2.cloned.1.call-update) | async-done | bytes 8388624 | tf_op jit(solution)/shard_map/all_gather | solution.py:44
  83.6 18.9 %convolution_bitcast_fusion = f32[1,16,8,64,1024]{4,3,1,2,0:T(8,128)} fusion(bf16[4,8,1024,128]{3,2,0,1:T(8,128)(2,1)} %all-gather.2.cloned.1.call-done, bf16[16,4,64,128]{3,2,1,0:T(8,128)(2,1)} %param.7, bf16[128]{0:T(256)(128)(2,1)S(1)} %convert_element_type.66), kind=kOutput, calls=%fused_computation | convolution fusion | flops 8592031744 | bytes 42991872 | tf_op jit(solution)/shard_map/ikac,kjbc->ijab/dot_general | solution.py:41
  102.5 3.2 fusion.17
  105.7 3.2 fusion.16
  108.9 3.2 fusion.15
  112.0 3.2 fusion.14
  115.2 3.2 fusion.13
  118.4 3.1 fusion.12
  121.5 3.2 fusion.11
  124.7 3.1 fusion.10
  127.8 3.2 fusion.9
  131.0 3.2 fusion.8
  134.2 3.1 fusion.7
  137.4 3.1 fusion.6
  140.5 3.2 fusion.5
  143.7 3.1 fusion.4
  146.8 3.2 fusion.3
  150.0 3.2 fusion.2
  153.2 369.4 %all_to_all.14 = f32[16,1,1,8,64,1024]{5,4,3,2,1,0:T(8,128)S(1)} all-to-all(f32[16,1,1,8,64,1024]{5,4,3,2,1,0:T(8,128)} %fusion.2), channel_id=1, replica_groups=mesh['row'=16,'col'=8] {'row'}, dimensions={0} | all-to-all | bytes 67108864 | tf_op jit(solution)/shard_map/all_to_all | solution.py:12
  522.6 11.0 %copy.57 = f32[1,1,8,16,64,1024]{5,4,3,2,1,0:T(8,128)} copy(f32[1,1,8,16,64,1024]{5,4,2,1,0,3:T(8,128)S(1)} %bitcast.125) | data formatting | bytes 67108864 | tf_op jit(solution)/shard_map/reshape | solution.py:13
  533.6 8.9 all-to-all-start.1
  542.6 0.0 copy-start
  543.9 362.2 %all-to-all-done.1 = f32[1,1,8,1024,1024]{4,3,1,0,2:T(8,128)} async-done(((f32[1,1,8,1024,1024]{4,3,1,0,2:T(8,128)}), f32[1,1,8,1024,1024]{4,3,1,0,2:T(8,128)}, u32[]{:S(2)}, u32[]{:S(2)}) %all-to-all-start.1) | async-done | bytes 33554464 | tf_op jit(solution)/shard_map/all_to_all | solution.py:47
  906.1 12.9 %reduce_sum.9 = bf16[1024,1024]{1,0:T(8,128)(2,1)S(1)} reduce(f32[1,1,8,1024,1024]{4,3,1,0,2:T(8,128)} %all-to-all-done.1, f32[]{:T(128)} %constant.16.clone.1), dimensions={0,1,2}, to_apply=%region_0.0 | reduce | flops 7340032 | bytes 35651588 | tf_op jit(solution)/shard_map/reduce_sum | solution.py:54
  919.0 0.0 copy-done
  919.0 2.3 fusion.1
Async XLA Ops:
  6.5 77.1 %all-gather.2.cloned.1.call-start = ((), (), s32[]{:S(2)}) async-start(), calls=%async_computation.2 | async-start | bytes 8912896 | tf_op jit(solution)/shard_map/all_gather | solution.py:44
  533.6 372.4 %all-to-all-start.1 = ((f32[1,1,8,1024,1024]{4,3,1,0,2:T(8,128)}), f32[1,1,8,1024,1024]{4,3,1,0,2:T(8,128)}, u32[]{:S(2)}, u32[]{:S(2)}) async-start(f32[1,1,8,1024,1024]{4,3,1,0,2:T(8,128)} %bitcast.124), calls=%async_computation.1 | async-start | bytes 67108864 | tf_op jit(solution)/shard_map/all_to_all | solution.py:47
  542.6 376.4 %copy-start = (f32[1024]{0:T(1024)S(1)}, f32[1024]{0:T(1024)}, u32[]{:S(2)}) copy-start(f32[1024]{0:T(1024)} %param.13) | copy-start | bytes 12292
Sparse Core Ops, SparseCore 0:
  9.5 74.0 all-gather.1
